TPU v7x, 256 devices: a whole 4x4x8 slice. The times are simulated.
256 devices in a mesh: row: 8 (over x, core), col: 16 (over y_lo, z), kern: 2 (over y_hi).
Axes of the slice: x: 4, y: 4 (y_hi: 2, y_lo: 2; y = y_hi * 2 + y_lo), z: 8, core: 2. Of those that a mesh axis runs over, the one named last changes fastest.
Arguments:
- mask_levels: int32 [256, 8192], P('row', 'col'), may hold values from 0 to 3
- level_offset: float32 [256, 8192], P('row', 'col'), may hold values from -6 to 6
- target_bits: int32 [256, 8192], P('row', 'col'), may hold values 0 or 1
- socs_kernels: bfloat16 [2, 24, 35, 35], P(None, 'kern'), may hold values from -0.067871094 to 0.067871094
- kernel_weights: float32 [24], P('kern'), may hold values from 0.1 to 1
Outputs:
- resist_image: float32 [256, 8192], P('row', 'col')
- mask_gradient: float32 [256, 8192], P('row', 'col')
All inputs are finite; a program needn't handle non-finite values. No bound on the sum of `target_bits` on one device may be relied on, other than what follows from the above.
Results may differ from a plain program's by a relative error of at most 0.0039.
Values may be sent and summed in bfloat16 or wider, within the bound.
No kernel may reach another device: no remote copies, remote signals or barrier semaphores. Data moves between devices by JAX's collectives and lax.ppermute only.
A program may use at most 64 MiB of HBM per device.

v0:
```python
import jax
import jax.numpy as jnp
from jax import lax
from jax.sharding import PartitionSpec as P

steepness = 4.0
threshold = 1.0
loss_gain = 32.0


def padded_2(value, sides, width):
    for axis, dim in sides:
        size, length = (lax.axis_size(axis), value.shape[dim])
        up = [(i, (i + 1) % size) for i in range(size - 1)]
        down = [(j, i) for i, j in up]
        last = lax.slice_in_dim(value, length - width, length, axis=dim)
        first = lax.slice_in_dim(value, 0, width, axis=dim)
        before = lax.ppermute(last, axis, up)
        after = lax.ppermute(first, axis, down)
        value = jnp.concatenate([before, value, after], axis=dim)
    return value


def column_windows(padded, blocks, reach):
    leading = padded.shape[:-1]
    central = padded[..., : blocks * 128].reshape(leading + (blocks, 128))
    filler = jnp.zeros(leading + (128 - reach,), padded.dtype)
    longer = jnp.concatenate([padded, filler], axis=-1)
    trailing = longer[..., 128:].reshape(leading + (blocks, 128))[..., :reach]
    return jnp.concatenate([central, trailing], axis=-1)


def band_select(stencil):
    window = 128 + stencil - 1
    offsets = (
        jnp.arange(window, dtype=jnp.int32)[:, None, None]
        - jnp.arange(128, dtype=jnp.int32)[None, :, None]
    )
    return (offsets == jnp.arange(stencil, dtype=jnp.int32)[None, None, :]).astype(jnp.bfloat16)


def forward_row(select, kernels, tap_row):
    kernel_row = lax.dynamic_index_in_dim(kernels, tap_row, 2, keepdims=False)
    toeplitz = jnp.einsum("job,ckb->jcko", select, kernel_row, preferred_element_type=jnp.float32)
    return toeplitz.astype(jnp.bfloat16).reshape(select.shape[0], -1)


def adjoint_row(select, flipped, tap_row):
    kernel_row = lax.dynamic_index_in_dim(flipped, tap_row, 2, keepdims=False)
    toeplitz = jnp.einsum("job,ckb->ckjo", select, kernel_row, preferred_element_type=jnp.float32)
    return toeplitz.astype(jnp.bfloat16).reshape(2 * flipped.shape[1], select.shape[0], 128)


def resist_terms(intensity, target):
    resist = jax.nn.sigmoid(steepness * (intensity - threshold))
    slope_term = (
        loss_gain * steepness * (resist - target.astype(jnp.float32)) * resist * (1.0 - resist)
    )
    return (resist, slope_term)


def per_device(mask_levels, level_offset, target_bits, socs_kernels, kernel_weights):
    tile_rows, tile_cols = mask_levels.shape
    stencil = socs_kernels.shape[-1]
    margin = stencil // 2
    reach = 2 * margin
    blocks = tile_cols // 128
    local_kernels = socs_kernels.shape[1]
    channels = 2 * local_kernels
    select = band_select(stencil)
    flipped = socs_kernels[:, :, ::-1, ::-1]
    mask_full = jax.nn.sigmoid(2.0 * (mask_levels.astype(jnp.float32) - 1.5) + level_offset)
    mask_bf = mask_full.astype(jnp.bfloat16)
    padded = padded_2(mask_bf, (("row", 0), ("col", 1)), margin)
    windows = column_windows(padded, blocks, reach)

    def forward_step(tap_row, running):
        row_slab = lax.dynamic_slice_in_dim(windows, tap_row, tile_rows, 0)
        weights_row = forward_row(select, socs_kernels, tap_row)
        return running + jnp.einsum(
            "xnj,jf->xnf", row_slab, weights_row, preferred_element_type=jnp.float32
        )

    fields = lax.fori_loop(
        0, stencil, forward_step, jnp.zeros((tile_rows, blocks, channels * 128), jnp.float32)
    )
    fields = fields.reshape(tile_rows, blocks, 2, local_kernels, 128)
    partial_value = jnp.sum(
        fields * fields * kernel_weights[None, None, None, :, None], axis=(2, 3)
    )
    partial_value = partial_value.reshape(tile_rows, tile_cols)
    intensity = lax.psum(partial_value, "kern")
    resist, slope_term = resist_terms(intensity, target_bits)
    scaled = (
        2.0
        * kernel_weights[None, None, None, :, None]
        * slope_term.reshape(tile_rows, blocks, 1, 1, 128)
    )
    charge = (scaled * fields).astype(jnp.bfloat16)
    charge = jnp.transpose(charge, (2, 3, 0, 1, 4)).reshape(channels, tile_rows, tile_cols)
    charge_padded = padded_2(charge, (("row", 1), ("col", 2)), margin)
    charge_windows = column_windows(charge_padded, blocks, reach)

    def adjoint_step(tap_row, running):
        row_slab = lax.dynamic_slice_in_dim(charge_windows, tap_row, tile_rows, 1)
        weights_row = adjoint_row(select, flipped, tap_row)
        return running + jnp.einsum(
            "cxnj,cjo->xno", row_slab, weights_row, preferred_element_type=jnp.float32
        )

    gradient_part = lax.fori_loop(
        0, stencil, adjoint_step, jnp.zeros((tile_rows, blocks, 128), jnp.float32)
    )
    gradient_part = gradient_part.reshape(tile_rows, tile_cols)
    summed = lax.psum(gradient_part, "kern")
    return (resist, summed * mask_full * (1.0 - mask_full))


def solution(mesh):
    return jax.shard_map(
        per_device,
        mesh=mesh,
        in_specs=(
            P("row", "col"),
            P("row", "col"),
            P("row", "col"),
            P(None, "kern", None, None),
            P("kern"),
        ),
        out_specs=(P("row", "col"), P("row", "col")),
        check_vma=False,
    )
```

profile of v0, /device:TPU:1, one launch (start us, length us, event | category | flops | bytes accessed | tf_op | source)
XLA Modules:
  0.0 472.6 jit_solution(10960512505497129558)
XLA Ops:
  8.1 4.5 collective-permute-start
  14.6 3.2 collective-permute-done.1
  17.9 3.5 collective-permute-start.2
  26.4 157.3 %while.28 = (s32[]{:T(128)}, f32[32,4,3072]{2,0,1:T(8,128)}, bf16[66,4,162]{2,0,1:T(8,128)(2,1)S(1)}, bf16[2,12,35,35]{3,1,0,2:T(8,128)(2,1)S(1)}, s32[162,128]{1,0:T(8,128)S(1)}, /*index=5*/s32[]{:T(128)}, s32[]{:T(128)}) while((s32[]{:T(128)}, f32[32,4,3072]{2,0,1:T(8,128)}, bf16[66,4,162]{2,0,1:T(8,128)(2,1)S(1)}, ...), condition=%wide.region_1.2_spmd.clone, body=%wide.region_0.1_spmd.clone.sunk | while | flops 164974080 | bytes 9314399 | solution.py:84
  62.8 3.0 convolution_add_fusion.2
  67.3 3.0 convolution_add_fusion.2
  71.8 3.0 convolution_add_fusion.2
  76.4 3.0 convolution_add_fusion.2
  80.9 3.0 convolution_add_fusion.2
  85.5 3.0 convolution_add_fusion.2
  90.0 3.0 convolution_add_fusion.2
  94.5 3.0 convolution_add_fusion.2
  99.1 3.0 convolution_add_fusion.2
  103.6 3.0 convolution_add_fusion.2
  108.1 3.0 convolution_add_fusion.2
  112.7 3.0 convolution_add_fusion.2
  117.2 3.0 convolution_add_fusion.2
  121.7 3.0 convolution_add_fusion.2
  126.3 3.0 convolution_add_fusion.2
  130.8 3.0 convolution_add_fusion.2
  135.3 3.0 convolution_add_fusion.2
  162.5 3.0 convolution_add_fusion.2
  186.8 36.1 %all-reduce.3.cloned.1.call-done = f32[32,512]{1,0:T(8,128)} async-done(((f32[32,512]{1,0:T(8,128)}), f32[32,512]{1,0:T(8,128)}) %all-reduce.3.cloned.1.call-update) | async-done | bytes 65552 | tf_op jit(solution)/shard_map/psum | solution.py:92
  226.4 4.1 collective-permute-start.4
  235.6 4.4 collective-permute-done.5
  241.1 3.2 collective-permute-start.6
  246.8 3.1 collective-permute-done.6
  253.5 6.0 %pad_maximum_fusion.4 = (bf16[24,66,512]{2,1,0:T(8,128)(2,1)S(1)}, bf16[24,66,512]{2,1,0:T(8,128)(2,1)}) fusion(bf16[24,66,17]{2,1,0:T(8,128)(2,1)} %copy-done.1, bf16[24,17,512]{2,1,0:T(8,128)(2,1)} %copy-done, bf16[24,32,512]{2,1,0:T(8,128)(2,1)S(1)} %reshape.72, bf16[24,17,512]{2,1,0:T(8,128)(2,1)S(1)} %copy.51, bf16[512]{0:T(512)(128)(2,1)S(1)} %pad_slice_fusion, ...), kind=kLoop, calls=%fused_computation.36 | loop fusion | flops 14598144 | bytes 4974784 | tf_op jit(solution)/shard_map/concatenate | solution.py:20
  259.5 3.7 reshape.86
  265.2 5.5 %pad_maximum_fusion = bf16[24,66,4,162]{3,2,1,0:T(4,128)(2,1)} fusion(bf16[24,66,4,34]{3,2,1,0:T(4,128)(2,1)} %bitcast.76, bf16[24,66,4,128]{3,2,1,0:T(4,128)(2,1)} %reshape.85), kind=kLoop, calls=%fused_computation.29 | loop fusion | flops 4105728 | bytes 4105728 | tf_op jit(solution)/shard_map/concatenate | solution.py:30
  270.8 155.4 %while.29 = (s32[]{:T(128)}, f32[32,4,128]{2,0,1:T(8,128)S(1)}, bf16[24,66,4,162]{3,2,1,0:T(4,128)(2,1)}, bf16[2,12,35,35]{3,1,0,2:T(8,128)(2,1)}, s32[162,128]{1,0:T(8,128)S(1)}, /*index=5*/s32[]{:T(128)}, s32[]{:T(128)}) while((s32[]{:T(128)}, f32[32,4,128]{2,0,1:T(8,128)S(1)}, bf16[24,66,4,162]{3,2,1,0:T(4,128)(2,1)}, ...), condition=%wide.region_5.6_spmd.clone, body=%wide.region_4.5_spmd.clone.sunk | while | flops 164220416 | bytes 7190107 | solution.py:111
  426.9 37.4 %all-reduce.5.cloned.1.call-done = f32[32,512]{1,0:T(8,128)} async-done(((f32[32,512]{1,0:T(8,128)}), f32[32,512]{1,0:T(8,128)}) %all-reduce.5.cloned.1.call-update) | async-done | bytes 65552 | tf_op jit(solution)/shard_map/psum | solution.py:115
  (322 shorter events, 286.9 us)
Async XLA Ops:
  7.2 215.7 %all-reduce.3.cloned.1.call-start = ((), (), s32[]{:S(2)}) async-start(), calls=%async_computation | async-start | bytes 131072 | tf_op jit(solution)/shard_map/psum | solution.py:92
  8.1 6.5 %collective-permute-start = (bf16[17,512]{1,0:T(8,128)(2,1)S(1)}, bf16[17,512]{1,0:T(8,128)(2,1)S(1)}, u32[]{:S(2)}, u32[]{:S(2)}) collective-permute-start(bf16[17,512]{1,0:T(8,128)(2,1)S(1)} %get-tuple-element.301), channel_id=1, source_target_pairs={{0,32},{32,64},{64,96},{96,128},{128,160},{160,192},{192,224},{1,3... | collective-permute-start | bytes 52232 | tf_op jit(solution)/shard_map/ppermute | solution.py:18
  12.7 5.1 %collective-permute-start.1 = (bf16[17,512]{1,0:T(8,128)(2,1)S(1)}, bf16[17,512]{1,0:T(8,128)(2,1)S(1)}, u32[]{:S(2)}, u32[]{:S(2)}) collective-permute-start(bf16[17,512]{1,0:T(8,128)(2,1)S(1)} %get-tuple-element.302), channel_id=1, source_target_pairs={{32,0},{64,32},{96,64},{128,96},{160,128},{192,160},{224,192},{33,... | collective-permute-start | bytes 52232 | tf_op jit(solution)/shard_map/ppermute | solution.py:19
  17.9 5.9 %collective-permute-start.2 = (bf16[66,17]{1,0:T(8,128)(2,1)S(1)}, bf16[66,17]{1,0:T(8,128)(2,1)S(1)}, u32[]{:S(2)}, u32[]{:S(2)}) collective-permute-start(bf16[66,17]{1,0:T(8,128)(2,1)S(1)} %get-tuple-element.299), channel_id=1, source_target_pairs={{0,2},{2,4},{4,6},{6,8},{8,10},{10,12},{12,14},{14,16},{16,18},{18... | collective-permute-start | bytes 6740 | tf_op jit(solution)/shard_map/ppermute | solution.py:18
  21.4 4.7 collective-permute-start.3
  183.7 1.7 copy-start.5
  185.4 37.5 %copy-start.4 = (s32[32,512]{1,0:T(8,128)S(1)}, s32[32,512]{1,0:T(8,128)}, u32[]{:S(2)}) copy-start(s32[32,512]{1,0:T(8,128)} %param.11) | copy-start | bytes 196612
  186.7 277.6 %all-reduce.5.cloned.1.call-start = ((), (), s32[]{:S(2)}) async-start(), calls=%async_computation.1 | async-start | bytes 131072 | tf_op jit(solution)/shard_map/psum | solution.py:115
  226.4 9.1 %collective-permute-start.4 = (bf16[24,17,512]{2,0,1:T(8,128)(2,1)S(1)}, bf16[24,17,512]{2,0,1:T(8,128)(2,1)S(1)}, u32[]{:S(2)}, u32[]{:S(2)}) collective-permute-start(bf16[24,17,512]{2,0,1:T(8,128)(2,1)S(1)} %copy.49), channel_id=1, source_target_pairs={{0,32},{32,64},{64,96},{96,128},{128,160},{160,192},{192,224},{1,3... | collective-permute-start | bytes 1253384 | tf_op jit(solution)/shard_map/ppermute | solution.py:18
  230.6 9.4 %collective-permute-start.5 = (bf16[24,17,512]{2,0,1:T(8,128)(2,1)S(1)}, bf16[24,17,512]{2,0,1:T(8,128)(2,1)S(1)}, u32[]{:S(2)}, u32[]{:S(2)}) collective-permute-start(bf16[24,17,512]{2,0,1:T(8,128)(2,1)S(1)} %copy.50), channel_id=1, source_target_pairs={{32,0},{64,32},{96,64},{128,96},{160,128},{192,160},{224,192},{33,... | collective-permute-start | bytes 1253384 | tf_op jit(solution)/shard_map/ppermute | solution.py:19
  240.1 9.8 %copy-start = (bf16[24,17,512]{2,1,0:T(8,128)(2,1)}, bf16[24,17,512]{2,1,0:T(8,128)(2,1)S(1)}, u32[]{:S(2)}) copy-start(bf16[24,17,512]{2,1,0:T(8,128)(2,1)S(1)} %copy.52) | copy-start | bytes 1253380
  241.1 8.7 %collective-permute-start.6 = (bf16[24,66,17]{2,1,0:T(8,128)(2,1)}, bf16[24,66,17]{2,1,0:T(8,128)(2,1)S(1)}, u32[]{:S(2)}, u32[]{:S(2)}) collective-permute-start(bf16[24,66,17]{2,1,0:T(8,128)(2,1)} %get-tuple-element.293), channel_id=1, source_target_pairs={{0,2},{2,4},{4,6},{6,8},{8,10},{10,12},{12,14},{14,16},{16,18},{18... | collective-permute-start | bytes 161576 | tf_op jit(solution)/shard_map/ppermute | solution.py:18
  244.3 9.2 %collective-permute-start.7 = (bf16[24,66,17]{2,1,0:T(8,128)(2,1)S(1)}, bf16[24,66,17]{2,1,0:T(8,128)(2,1)}, u32[]{:S(2)}, u32[]{:S(2)}) collective-permute-start(bf16[24,66,17]{2,1,0:T(8,128)(2,1)S(1)} %get-tuple-element.294), channel_id=1, source_target_pairs={{2,0},{4,2},{6,4},{8,6},{10,8},{12,10},{14,12},{16,14},{18,16},{20... | collective-permute-start | bytes 161576 | tf_op jit(solution)/shard_map/ppermute | solution.py:19
  249.9 0.8 copy-start.1
  270.8 193.5 %copy-start.2 = (f32[32,512]{1,0:T(8,128)S(1)}, f32[32,512]{1,0:T(8,128)}, u32[]{:S(2)}) copy-start(f32[32,512]{1,0:T(8,128)} %param.10) | copy-start | bytes 196612
  270.8 193.5 %copy-start.3 = (s32[32,512]{1,0:T(8,128)S(1)}, s32[32,512]{1,0:T(8,128)}, u32[]{:S(2)}) copy-start(s32[32,512]{1,0:T(8,128)} %param.9) | copy-start | bytes 196612
Sparse Core Ops, SparseCore 0:
  186.8 36.0 all-reduce.2
  427.0 37.2 all-reduce.4
where the time goes:
time: 477 us; the launch traced here: 473 us
  matrix products  192 us (40%)
  local copies, waits for them, and re-layouts  132 us (28%)
  waiting for transfers between devices  92.3 us (19%)
  starting transfers between devices  22 us (5%)
  other arithmetic  18 us (4%)
  between operations  14.3 us (3%)
    dot_general x35, matrix products, forward_step(): jnp.einsum('xnj,jf->xnf', row_slab, weights_row, preferred_element_type=j...  103 us
    dynamic_slice x35, local copies, waits for them, and re-layouts, adjoint_step(): row_slab = lax.dynamic_slice_in_dim(charge_windows, tap_row, tile_rows, 1)  77.8 us
    dot_general x35, matrix products, adjoint_row(): jnp.einsum('job,ckb->ckjo', select, kernel_row, preferred_element_type=jn...  46.3 us
    psum x1, waiting for transfers between devices, per_device(): summed = lax.psum(gradient_part, 'kern')  37.4 us
    psum x1, waiting for transfers between devices, per_device(): intensity = lax.psum(partial_value, 'kern')  36.1 us
    reshape x35, local copies, waits for them, and re-layouts, forward_row(): return toeplitz.astype(jnp.bfloat16).reshape(select.shape[0], -1)  23.3 us
    dot_general x35, matrix products, forward_row(): jnp.einsum('job,ckb->jcko', select, kernel_row, preferred_element_type=jn...  21.6 us
    dot_general x35, matrix products, adjoint_step(): jnp.einsum('cxnj,cjo->xno', row_slab, weights_row, preferred_element_type...  20.4 us
  transfers between devices with their start and end apart: 10, of which 8 were waited for; matrix products, arithmetic and copies ran while one was open for 0% of the time, Pallas kernels for 0%

commit v1 on v0

--- a/solution.py
+++ b/solution.py
@@ -112,7 +112,7 @@
         0, stencil, adjoint_step, jnp.zeros((tile_rows, blocks, 128), jnp.float32)
     )
     gradient_part = gradient_part.reshape(tile_rows, tile_cols)
-    summed = lax.psum(gradient_part, "kern")
+    summed = jnp.sum(lax.all_gather(gradient_part, "kern"), axis=0)
     return (resist, summed * mask_full * (1.0 - mask_full))
 
 

time: 477 us -> 449 us (0.941)
  the two profiles are of different devices: /device:TPU:1 before, /device:TPU:100 now
where the time goes in v1:
time: 449 us; the launch traced here: 445 us
  matrix products  192 us (43%)
  local copies, waits for them, and re-layouts  131 us (29%)
  waiting for transfers between devices  56.5 us (13%)
  starting transfers between devices  24.9 us (6%)
  other arithmetic  17.2 us (4%)
  between operations  14.3 us (3%)
  blocking collectives  6.45 us (1%)
    dot_general x35, matrix products, forward_step(): jnp.einsum('xnj,jf->xnf', row_slab, weights_row, preferred_element_type=j...  103 us
    dynamic_slice x35, local copies, waits for them, and re-layouts, adjoint_step(): row_slab = lax.dynamic_slice_in_dim(charge_windows, tap_row, tile_rows, 1)  77.8 us
    dot_general x35, matrix products, adjoint_row(): jnp.einsum('job,ckb->ckjo', select, kernel_row, preferred_element_type=jn...  46.3 us
    psum x1, waiting for transfers between devices, per_device(): intensity = lax.psum(partial_value, 'kern')  33.4 us
    reshape x35, local copies, waits for them, and re-layouts, forward_row(): return toeplitz.astype(jnp.bfloat16).reshape(select.shape[0], -1)  23.3 us
    dot_general x35, matrix products, forward_row(): jnp.einsum('job,ckb->jcko', select, kernel_row, preferred_element_type=jn...  21.6 us
    dot_general x35, matrix products, adjoint_step(): jnp.einsum('cxnj,cjo->xno', row_slab, weights_row, preferred_element_type...  20.4 us
    ppermute x4, starting transfers between devices, padded_2(): before = lax.ppermute(last, axis, up)  13.5 us
  transfers between devices with their start and end apart: 9, of which 7 were waited for; matrix products, arithmetic and copies ran while one was open for 1% of the time, Pallas kernels for 0%

profile of v1, /device:TPU:100, one launch (start us, length us, event | category | flops | bytes accessed | tf_op | source)
XLA Modules:
  0.0 444.8 jit_solution(4540591928133479722)
XLA Ops:
  10.1 3.6 collective-permute-start.1
  15.3 5.0 %collective-permute-start.2 = (bf16[66,17]{1,0:T(8,128)(2,1)S(1)}, bf16[66,17]{1,0:T(8,128)(2,1)S(1)}, u32[]{:S(2)}, u32[]{:S(2)}) collective-permute-start(bf16[66,17]{1,0:T(8,128)(2,1)S(1)} %get-tuple-element.299), channel_id=1, source_target_pairs={{0,2},{2,4},{4,6},{6,8},{8,10},{10,12},{12,14},{14,16},{16,18},{18... | collective-permute-start | bytes 6740 | tf_op jit(solution)/shard_map/ppermute | solution.py:18
  23.3 4.0 collective-permute-done.3
  27.6 157.3 %while.28 = (s32[]{:T(128)}, f32[32,4,3072]{2,0,1:T(8,128)}, bf16[66,4,162]{2,0,1:T(8,128)(2,1)S(1)}, bf16[2,12,35,35]{3,1,0,2:T(8,128)(2,1)S(1)}, s32[162,128]{1,0:T(8,128)S(1)}, /*index=5*/s32[]{:T(128)}, s32[]{:T(128)}) while((s32[]{:T(128)}, f32[32,4,3072]{2,0,1:T(8,128)}, bf16[66,4,162]{2,0,1:T(8,128)(2,1)S(1)}, ...), condition=%wide.region_1.2_spmd.clone, body=%wide.region_0.1_spmd.clone.sunk | while | flops 164974080 | bytes 9314399 | solution.py:84
  64.0 3.0 convolution_add_fusion.2
  68.5 3.0 convolution_add_fusion.2
  73.1 3.0 convolution_add_fusion.2
  77.6 3.0 convolution_add_fusion.2
  82.1 3.0 convolution_add_fusion.2
  86.7 3.0 convolution_add_fusion.2
  91.2 3.0 convolution_add_fusion.2
  95.7 3.0 convolution_add_fusion.2
  100.3 3.0 convolution_add_fusion.2
  104.8 3.0 convolution_add_fusion.2
  109.3 3.0 convolution_add_fusion.2
  113.9 3.0 convolution_add_fusion.2
  118.4 3.0 convolution_add_fusion.2
  122.9 3.0 convolution_add_fusion.2
  127.5 3.0 convolution_add_fusion.2
  132.0 3.0 convolution_add_fusion.2
  159.2 3.0 convolution_add_fusion.2
  187.9 33.4 %all-reduce.2.cloned.1.call-done = f32[32,512]{1,0:T(8,128)} async-done(((f32[32,512]{1,0:T(8,128)}), f32[32,512]{1,0:T(8,128)}) %all-reduce.2.cloned.1.call-update) | async-done | bytes 65552 | tf_op jit(solution)/shard_map/psum | solution.py:92
  226.9 3.6 collective-permute-start.5
  230.5 3.6 collective-permute-done.4
  237.3 4.7 %collective-permute-start.6 = (bf16[24,66,17]{2,1,0:T(8,128)(2,1)}, bf16[24,66,17]{2,1,0:T(8,128)(2,1)S(1)}, u32[]{:S(2)}, u32[]{:S(2)}) collective-permute-start(bf16[24,66,17]{2,1,0:T(8,128)(2,1)} %get-tuple-element.293), channel_id=1, source_target_pairs={{0,2},{2,4},{4,6},{6,8},{8,10},{10,12},{12,14},{14,16},{16,18},{18... | collective-permute-start | bytes 161576 | tf_op jit(solution)/shard_map/ppermute | solution.py:18
  245.0 7.4 %collective-permute-done.6 = bf16[24,66,17]{2,1,0:T(8,128)(2,1)S(1)} collective-permute-done((bf16[24,66,17]{2,1,0:T(8,128)(2,1)}, bf16[24,66,17]{2,1,0:T(8,128)(2,1)S(1)}, u32[]{:S(2)}, u32[]{:S(2)}) %collective-permute-start.6) | collective-permute-done | bytes 53888 | tf_op jit(solution)/shard_map/ppermute | solution.py:18
  253.1 4.8 %collective-permute-done.7 = bf16[24,66,17]{2,1,0:T(8,128)(2,1)} collective-permute-done((bf16[24,66,17]{2,1,0:T(8,128)(2,1)S(1)}, bf16[24,66,17]{2,1,0:T(8,128)(2,1)}, u32[]{:S(2)}, u32[]{:S(2)}) %collective-permute-start.7) | collective-permute-done | bytes 53888 | tf_op jit(solution)/shard_map/ppermute | solution.py:19
  258.0 6.0 %pad_maximum_fusion.4 = (bf16[24,66,512]{2,1,0:T(8,128)(2,1)S(1)}, bf16[24,66,512]{2,1,0:T(8,128)(2,1)}) fusion(bf16[24,66,17]{2,1,0:T(8,128)(2,1)} %copy-done.1, bf16[24,17,512]{2,1,0:T(8,128)(2,1)} %copy-done, bf16[24,32,512]{2,1,0:T(8,128)(2,1)S(1)} %reshape.69, bf16[24,17,512]{2,1,0:T(8,128)(2,1)S(1)} %copy.50, bf16[512]{0:T(512)(128)(2,1)S(1)} %pad_slice_fusion, ...), kind=kLoop, calls=%fused_computation.36 | loop fusion | flops 14598144 | bytes 4974784 | tf_op jit(solution)/shard_map/concatenate | solution.py:20
  264.0 3.7 reshape.82
  269.7 5.5 %pad_maximum_fusion = bf16[24,66,4,162]{3,2,1,0:T(4,128)(2,1)} fusion(bf16[24,66,4,34]{3,2,1,0:T(4,128)(2,1)} %bitcast.71, bf16[24,66,4,128]{3,2,1,0:T(4,128)(2,1)} %reshape.81), kind=kLoop, calls=%fused_computation.29 | loop fusion | flops 4105728 | bytes 4105728 | tf_op jit(solution)/shard_map/concatenate | solution.py:30
  275.2 155.4 %while.29 = (s32[]{:T(128)}, f32[32,4,128]{2,0,1:T(8,128)S(1)}, bf16[24,66,4,162]{3,2,1,0:T(4,128)(2,1)}, bf16[2,12,35,35]{3,1,0,2:T(8,128)(2,1)}, s32[162,128]{1,0:T(8,128)S(1)}, /*index=5*/s32[]{:T(128)}, s32[]{:T(128)}) while((s32[]{:T(128)}, f32[32,4,128]{2,0,1:T(8,128)S(1)}, bf16[24,66,4,162]{3,2,1,0:T(4,128)(2,1)}, ...), condition=%wide.region_5.6_spmd.clone, body=%wide.region_4.5_spmd.clone.sunk | while | flops 164220416 | bytes 7190107 | solution.py:111
  430.8 6.4 %all_gather.3 = f32[2,32,512]{2,1,0:T(8,128)S(1)} all-gather(f32[1,32,512]{2,1,0:T(8,128)S(1)} %all_gather_reshape.3), channel_id=1, replica_groups=mesh['row'=8,'col'=16,'kern'=2] {'kern'}, dimensions={0}, use_global_device_ids=true | all-gather | bytes 196608 | tf_op jit(solution)/shard_map/all_gather | solution.py:115
  (322 shorter events, 284.9 us)
Async XLA Ops:
  7.2 214.2 %all-reduce.2.cloned.1.call-start = ((), (), s32[]{:S(2)}) async-start(), calls=%async_computation | async-start | bytes 131072 | tf_op jit(solution)/shard_map/psum | solution.py:92
  8.1 5.6 %collective-permute-start = (bf16[17,512]{1,0:T(8,128)(2,1)S(1)}, bf16[17,512]{1,0:T(8,128)(2,1)S(1)}, u32[]{:S(2)}, u32[]{:S(2)}) collective-permute-start(bf16[17,512]{1,0:T(8,128)(2,1)S(1)} %get-tuple-element.301), channel_id=1, source_target_pairs={{0,32},{32,64},{64,96},{96,128},{128,160},{160,192},{192,224},{1,3... | collective-permute-start | bytes 52232 | tf_op jit(solution)/shard_map/ppermute | solution.py:18
  10.1 5.1 %collective-permute-start.1 = (bf16[17,512]{1,0:T(8,128)(2,1)S(1)}, bf16[17,512]{1,0:T(8,128)(2,1)S(1)}, u32[]{:S(2)}, u32[]{:S(2)}) collective-permute-start(bf16[17,512]{1,0:T(8,128)(2,1)S(1)} %get-tuple-element.302), channel_id=1, source_target_pairs={{32,0},{64,32},{96,64},{128,96},{160,128},{192,160},{224,192},{33,... | collective-permute-start | bytes 52232 | tf_op jit(solution)/shard_map/ppermute | solution.py:19
  15.3 8.0 %collective-permute-start.2 = (bf16[66,17]{1,0:T(8,128)(2,1)S(1)}, bf16[66,17]{1,0:T(8,128)(2,1)S(1)}, u32[]{:S(2)}, u32[]{:S(2)}) collective-permute-start(bf16[66,17]{1,0:T(8,128)(2,1)S(1)} %get-tuple-element.299), channel_id=1, source_target_pairs={{0,2},{2,4},{4,6},{6,8},{8,10},{10,12},{12,14},{14,16},{16,18},{18... | collective-permute-start | bytes 6740 | tf_op jit(solution)/shard_map/ppermute | solution.py:18
  20.3 7.0 %collective-permute-start.3 = (bf16[66,17]{1,0:T(8,128)(2,1)S(1)}, bf16[66,17]{1,0:T(8,128)(2,1)S(1)}, u32[]{:S(2)}, u32[]{:S(2)}) collective-permute-start(bf16[66,17]{1,0:T(8,128)(2,1)S(1)} %get-tuple-element.300), channel_id=1, source_target_pairs={{2,0},{4,2},{6,4},{8,6},{10,8},{12,10},{14,12},{16,14},{18,16},{20... | collective-permute-start | bytes 6740 | tf_op jit(solution)/shard_map/ppermute | solution.py:19
  184.9 1.7 copy-start.5
  186.6 34.7 %copy-start.4 = (s32[32,512]{1,0:T(8,128)S(1)}, s32[32,512]{1,0:T(8,128)}, u32[]{:S(2)}) copy-start(s32[32,512]{1,0:T(8,128)} %param.11) | copy-start | bytes 196612
  224.8 9.4 %collective-permute-start.4 = (bf16[24,17,512]{2,0,1:T(8,128)(2,1)S(1)}, bf16[24,17,512]{2,0,1:T(8,128)(2,1)S(1)}, u32[]{:S(2)}, u32[]{:S(2)}) collective-permute-start(bf16[24,17,512]{2,0,1:T(8,128)(2,1)S(1)} %copy.48), channel_id=1, source_target_pairs={{0,32},{32,64},{64,96},{96,128},{128,160},{160,192},{192,224},{1,3... | collective-permute-start | bytes 1253384 | tf_op jit(solution)/shard_map/ppermute | solution.py:18
  226.9 9.2 %collective-permute-start.5 = (bf16[24,17,512]{2,0,1:T(8,128)(2,1)S(1)}, bf16[24,17,512]{2,0,1:T(8,128)(2,1)S(1)}, u32[]{:S(2)}, u32[]{:S(2)}) collective-permute-start(bf16[24,17,512]{2,0,1:T(8,128)(2,1)S(1)} %copy.49), channel_id=1, source_target_pairs={{32,0},{64,32},{96,64},{128,96},{160,128},{192,160},{224,192},{33,... | collective-permute-start | bytes 1253384 | tf_op jit(solution)/shard_map/ppermute | solution.py:19
  236.2 16.2 %copy-start = (bf16[24,17,512]{2,1,0:T(8,128)(2,1)}, bf16[24,17,512]{2,1,0:T(8,128)(2,1)S(1)}, u32[]{:S(2)}) copy-start(bf16[24,17,512]{2,1,0:T(8,128)(2,1)S(1)} %copy.51) | copy-start | bytes 1253380
  237.3 15.1 %collective-permute-start.6 = (bf16[24,66,17]{2,1,0:T(8,128)(2,1)}, bf16[24,66,17]{2,1,0:T(8,128)(2,1)S(1)}, u32[]{:S(2)}, u32[]{:S(2)}) collective-permute-start(bf16[24,66,17]{2,1,0:T(8,128)(2,1)} %get-tuple-element.293), channel_id=1, source_target_pairs={{0,2},{2,4},{4,6},{6,8},{8,10},{10,12},{12,14},{14,16},{16,18},{18... | collective-permute-start | bytes 161576 | tf_op jit(solution)/shard_map/ppermute | solution.py:18
  241.9 16.1 %collective-permute-start.7 = (bf16[24,66,17]{2,1,0:T(8,128)(2,1)S(1)}, bf16[24,66,17]{2,1,0:T(8,128)(2,1)}, u32[]{:S(2)}, u32[]{:S(2)}) collective-permute-start(bf16[24,66,17]{2,1,0:T(8,128)(2,1)S(1)} %get-tuple-element.294), channel_id=1, source_target_pairs={{2,0},{4,2},{6,4},{8,6},{10,8},{12,10},{14,12},{16,14},{18,16},{20... | collective-permute-start | bytes 161576 | tf_op jit(solution)/shard_map/ppermute | solution.py:19
  252.4 0.8 copy-start.1
  275.2 162.0 %copy-start.2 = (f32[32,512]{1,0:T(8,128)S(1)}, f32[32,512]{1,0:T(8,128)}, u32[]{:S(2)}) copy-start(f32[32,512]{1,0:T(8,128)} %param.10) | copy-start | bytes 196612
  275.2 162.0 %copy-start.3 = (s32[32,512]{1,0:T(8,128)S(1)}, s32[32,512]{1,0:T(8,128)}, u32[]{:S(2)}) copy-start(s32[32,512]{1,0:T(8,128)} %param.9) | copy-start | bytes 196612
Sparse Core Ops, SparseCore 0:
  188.0 33.2 all-reduce.1
